TPU v7x, 128 devices: a whole 4x4x4 slice. The times are simulated.
128 devices in a mesh: gx: 16 (over y, x_hi, core), gy: 8 (over x_lo, z).
Axes of the slice: x: 4 (x_hi: 2, x_lo: 2; x = x_hi * 2 + x_lo), y: 4, z: 4, core: 2. Of those that a mesh axis runs over, the one named last changes fastest.
Arguments:
- mixing: float32 [3, 8, 128, 1024], P(None, None, 'gx', 'gy'), may hold values from 0.02 to 0.5
- forcing: float32 [2, 8, 128, 1024], P(None, None, 'gx', 'gy'), may hold values from -6 to 6
- labels: int32 [8, 128, 1024], P(None, 'gx', 'gy'), may hold values from 0 to 2
- colours: int32 [16, 8], P('gx', 'gy'), may hold values from 0 to 5
- coarse_basis: float32 [2, 8, 128, 1024], P(None, None, 'gx', 'gy'), may hold values from 0.5 to 2
- coarse_inverse: float32 [16, 8, 2, 256], P('gx', 'gy'), may hold values from -4 to 4
Outputs:
- concentration: float32 [2, 8, 128, 1024], P(None, None, 'gx', 'gy')
- coarse_coeff: float32 [16, 8, 2], P('gx', 'gy')
All inputs are finite; a program needn't handle non-finite values.
Results may differ from a plain program's by a relative error of at most 0.0003.
Values sent between devices are 32-bit elements; how exact they have to be, the bound alone decides.
No kernel may reach another device: no remote copies, remote signals or barrier semaphores. Data moves between devices by JAX's collectives and lax.ppermute only.
A program may use at most 64 MiB of HBM per device.

v0:
```python
import jax
import jax.numpy as jnp
from jax import lax
from jax.sharding import PartitionSpec as P

MARGIN = 4
SWEEPS = 20
ROUNDS = 6


ROBIN = 1.0
OMEGA = 0.8


def with_halo(cells, sides, width):
    for axis, dim in sides:
        count = lax.axis_size(axis)
        ends = count - 1
        head = lax.slice_in_dim(cells, 0, width, axis=dim)
        tail = lax.slice_in_dim(cells, cells.shape[dim] - width, cells.shape[dim], axis=dim)
        cells = jnp.concatenate(
            [
                lax.ppermute(tail, axis, [(i, (i + 1) % count) for i in range(ends)]),
                cells,
                lax.ppermute(head, axis, [((i + 1) % count, i) for i in range(ends)]),
            ],
            axis=dim,
        )
    return cells


def neighbour_op(padded, s11, s22, s12, diag):
    centre = padded[:, :, 1:-1, 1:-1]
    zpad = jnp.pad(centre, ((0, 0), (1, 1), (0, 0), (0, 0)))
    near = padded[:, :, 2:, 1:-1] + padded[:, :, :-2, 1:-1]
    near = near + padded[:, :, 1:-1, 2:] + padded[:, :, 1:-1, :-2]
    near = near + zpad[:, 2:] + zpad[:, :-2]
    first = s11 * centre[0] + s12 * centre[1] + diag * centre[0] - near[0]
    second = s12 * centre[0] + s22 * centre[1] + diag * centre[1] - near[1]
    return jnp.stack([first, second])


def margin_tables(first_x, first_y, ext_x, ext_y, total_x, total_y):
    index_x = jnp.arange(ext_x, dtype=jnp.int32)
    index_y = jnp.arange(ext_y, dtype=jnp.int32)
    cells_x = first_x - MARGIN + index_x
    cells_y = first_y - MARGIN + index_y
    in_x = (cells_x >= 0) & (cells_x < total_x)
    in_y = (cells_y >= 0) & (cells_y < total_y)
    inside = (in_x[:, None] & in_y[None, :]).astype(jnp.float32)
    rim_x = ((index_x == 0) & (cells_x - 1 >= 0)).astype(jnp.float32) + (
        (index_x == ext_x - 1) & (cells_x + 1 < total_x)
    ).astype(jnp.float32)
    rim_y = ((index_y == 0) & (cells_y - 1 >= 0)).astype(jnp.float32) + (
        (index_y == ext_y - 1) & (cells_y + 1 < total_y)
    ).astype(jnp.float32)
    count = rim_x[:, None] + rim_y[None, :]
    return (inside, count)


def local_solve(residual, s11, s22, s12, inside, count):
    diag = 6.0 + ROBIN * count
    scale = jnp.stack([s11 + diag, s22 + diag])
    correction = jnp.zeros_like(residual)
    for sweep in range(SWEEPS):
        padded = jnp.pad(correction, ((0, 0), (0, 0), (1, 1), (1, 1)))
        image = neighbour_op(padded, s11, s22, s12, diag)
        correction = (correction + OMEGA * (residual - image) / scale) * inside
    return correction


def couplings(mixing):
    return (mixing[0], mixing[1], 0.25 * (mixing[2] - 0.125))


def shards(mixing, forcing, labels, colours, coarse_basis, coarse_inverse):
    size_x = mixing.shape[2]
    size_y = mixing.shape[3]
    total_x = size_x * lax.axis_size("gx")
    total_y = size_y * lax.axis_size("gy")
    first_x = lax.axis_index("gx") * size_x
    first_y = lax.axis_index("gy") * size_y
    ext_x = size_x + 2 * MARGIN
    ext_y = size_y + 2 * MARGIN
    inside, count = margin_tables(first_x, first_y, ext_x, ext_y, total_x, total_y)
    s11, s22, s12 = couplings(mixing)
    onehot = jnp.stack([labels == 1, labels == 2]).astype(jnp.float32)
    rhs = onehot + forcing
    state = onehot
    wide_mix = with_halo(mixing, (("gx", 2), ("gy", 3)), MARGIN)
    m11, m22, m12 = couplings(wide_mix)
    for rnd in range(ROUNDS):
        faces = with_halo(state, (("gx", 2), ("gy", 3)), 1)
        own_res = rhs - neighbour_op(faces, s11, s22, s12, 6.0)
        local_res = with_halo(own_res, (("gx", 2), ("gy", 3)), MARGIN) * inside
        correction = local_solve(local_res, m11, m22, m12, inside, count)
        chosen = (colours[0, 0] == rnd).astype(jnp.float32)
        state = (
            state + correction[:, :, MARGIN : MARGIN + size_x, MARGIN : MARGIN + size_y] * chosen
        )
    faces = with_halo(state, (("gx", 2), ("gy", 3)), 1)
    residual = rhs - neighbour_op(faces, s11, s22, s12, 6.0)
    weighted = jnp.sum(coarse_basis * residual, axis=(1, 2, 3)) / (
        mixing.shape[1] * size_x * size_y
    )
    gathered = lax.all_gather(weighted.reshape(1, 2), ("gx", "gy"), axis=0, tiled=True)
    values = gathered.reshape(-1)
    coarse = jnp.dot(coarse_inverse[0, 0], values, precision=lax.Precision.HIGHEST)
    result = state + coarse_basis * coarse[:, None, None, None]
    return (result, coarse.reshape(1, 1, 2))


def solution(mesh):
    return jax.shard_map(
        shards,
        mesh=mesh,
        in_specs=(
            P(None, None, "gx", "gy"),
            P(None, None, "gx", "gy"),
            P(None, "gx", "gy"),
            P("gx", "gy"),
            P(None, None, "gx", "gy"),
            P("gx", "gy", None, None),
        ),
        out_specs=(P(None, None, "gx", "gy"), P("gx", "gy", None)),
        check_vma=False,
    )
```

profile of v0, /device:TPU:1, one launch (start us, length us, event | category | flops | bytes accessed | tf_op | source)
XLA Modules:
  0.0 449.3 jit_solution(3353353404357098089)
XLA Ops:
  24.2 5.8 %collective-permute-start.4 = (f32[2,8,4,128]{3,2,1,0:T(4,128)S(1)}, f32[2,8,4,128]{3,2,1,0:T(4,128)S(1)}, u32[]{:S(2)}, u32[]{:S(2)}) collective-permute-start(f32[2,8,4,128]{3,2,1,0:T(4,128)S(1)} %get-tuple-element.316), channel_id=1, source_target_pairs={{0,8},{8,16},{16,24},{24,32},{32,40},{40,48},{48,56},{56,64},{64,7... | collective-permute-start | bytes 98312 | tf_op jit(solution)/shard_map/ppermute | solution.py:23
  48.6 5.0 %collective-permute-done.7 = f32[2,8,16,4]{3,2,1,0:T(8,128)S(1)} collective-permute-done((f32[2,8,16,4]{3,2,1,0:T(8,128)S(1)}, f32[2,8,16,4]{3,2,1,0:T(8,128)S(1)}, u32[]{:S(2)}, u32[]{:S(2)}) %collective-permute-start.7) | collective-permute-done | bytes 4128 | tf_op jit(solution)/shard_map/ppermute | solution.py:25
  63.7 5.1 %collective-permute-start.13 = (f32[2,8,1,128]{3,2,1,0:T(1,128)S(1)}, f32[2,8,1,128]{3,2,1,0:T(1,128)S(1)}, u32[]{:S(2)}, u32[]{:S(2)}) collective-permute-start(f32[2,8,1,128]{3,2,1,0:T(1,128)S(1)} %get-tuple-element.314), channel_id=1, source_target_pairs={{0,8},{8,16},{16,24},{24,32},{32,40},{40,48},{48,56},{56,64},{64,7... | collective-permute-start | bytes 24584 | tf_op jit(solution)/shard_map/ppermute | solution.py:23
  71.1 6.2 %collective-permute-start.15 = (f32[2,8,10,1]{3,2,1,0:T(8,128)S(1)}, f32[2,8,10,1]{3,2,1,0:T(8,128)S(1)}, u32[]{:S(2)}, u32[]{:S(2)}) collective-permute-start(f32[2,8,10,1]{3,2,1,0:T(8,128)S(1)} %get-tuple-element.287), channel_id=1, source_target_pairs={{0,1},{1,2},{2,3},{3,4},{4,5},{5,6},{6,7},{8,9},{9,10},{10,11},{11... | collective-permute-start | bytes 1928 | tf_op jit(solution)/shard_map/ppermute | solution.py:23
  79.5 6.5 %collective-permute-start.16 = (f32[2,8,4,128]{3,2,1,0:T(4,128)S(1)}, f32[2,8,4,128]{3,2,1,0:T(4,128)S(1)}, u32[]{:S(2)}, u32[]{:S(2)}) collective-permute-start(f32[2,8,4,128]{3,2,1,0:T(4,128)S(1)} %get-tuple-element.312), channel_id=1, source_target_pairs={{0,8},{8,16},{16,24},{24,32},{32,40},{40,48},{48,56},{56,64},{64,7... | collective-permute-start | bytes 98312 | tf_op jit(solution)/shard_map/ppermute | solution.py:23
  92.9 5.5 %collective-permute-start.18 = (f32[2,8,16,4]{3,2,1,0:T(8,128)S(1)}, f32[2,8,16,4]{3,2,1,0:T(8,128)S(1)}, u32[]{:S(2)}, u32[]{:S(2)}) collective-permute-start(f32[2,8,16,4]{3,2,1,0:T(8,128)S(1)} %get-tuple-element.284), channel_id=1, source_target_pairs={{0,1},{1,2},{2,3},{3,4},{4,5},{5,6},{6,7},{8,9},{9,10},{10,11},{11... | collective-permute-start | bytes 12296 | tf_op jit(solution)/shard_map/ppermute | solution.py:23
  100.3 5.9 %collective-permute-done.19 = f32[2,8,16,4]{3,2,1,0:T(8,128)S(1)} collective-permute-done((f32[2,8,16,4]{3,2,1,0:T(8,128)S(1)}, f32[2,8,16,4]{3,2,1,0:T(8,128)S(1)}, u32[]{:S(2)}, u32[]{:S(2)}) %collective-permute-start.19) | collective-permute-done | bytes 4128 | tf_op jit(solution)/shard_map/ppermute | solution.py:25
  116.3 6.3 %collective-permute-start.21 = (f32[2,8,1,128]{3,2,1,0:T(1,128)S(1)}, f32[2,8,1,128]{3,2,1,0:T(1,128)S(1)}, u32[]{:S(2)}, u32[]{:S(2)}) collective-permute-start(f32[2,8,1,128]{3,2,1,0:T(1,128)S(1)} %get-tuple-element.310), channel_id=1, source_target_pairs={{0,8},{8,16},{16,24},{24,32},{32,40},{40,48},{48,56},{56,64},{64,7... | collective-permute-start | bytes 24584 | tf_op jit(solution)/shard_map/ppermute | solution.py:23
  124.8 6.4 %collective-permute-start.23 = (f32[2,8,10,1]{3,2,1,0:T(8,128)S(1)}, f32[2,8,10,1]{3,2,1,0:T(8,128)S(1)}, u32[]{:S(2)}, u32[]{:S(2)}) collective-permute-start(f32[2,8,10,1]{3,2,1,0:T(8,128)S(1)} %get-tuple-element.283), channel_id=1, source_target_pairs={{0,1},{1,2},{2,3},{3,4},{4,5},{5,6},{6,7},{8,9},{9,10},{10,11},{11... | collective-permute-start | bytes 1928 | tf_op jit(solution)/shard_map/ppermute | solution.py:23
  133.3 6.7 %collective-permute-start.24 = (f32[2,8,4,128]{3,2,1,0:T(4,128)S(1)}, f32[2,8,4,128]{3,2,1,0:T(4,128)S(1)}, u32[]{:S(2)}, u32[]{:S(2)}) collective-permute-start(f32[2,8,4,128]{3,2,1,0:T(4,128)S(1)} %get-tuple-element.308), channel_id=1, source_target_pairs={{0,8},{8,16},{16,24},{24,32},{32,40},{40,48},{48,56},{56,64},{64,7... | collective-permute-start | bytes 98312 | tf_op jit(solution)/shard_map/ppermute | solution.py:23
  142.0 4.8 %collective-permute-done.25 = f32[2,8,4,128]{3,2,1,0:T(4,128)S(1)} collective-permute-done((f32[2,8,4,128]{3,2,1,0:T(4,128)S(1)}, f32[2,8,4,128]{3,2,1,0:T(4,128)S(1)}, u32[]{:S(2)}, u32[]{:S(2)}) %collective-permute-start.25) | collective-permute-done | bytes 32800 | tf_op jit(solution)/shard_map/ppermute | solution.py:25
  146.9 6.8 %collective-permute-start.26 = (f32[2,8,16,4]{3,2,1,0:T(8,128)S(1)}, f32[2,8,16,4]{3,2,1,0:T(8,128)S(1)}, u32[]{:S(2)}, u32[]{:S(2)}) collective-permute-start(f32[2,8,16,4]{3,2,1,0:T(8,128)S(1)} %get-tuple-element.280), channel_id=1, source_target_pairs={{0,1},{1,2},{2,3},{3,4},{4,5},{5,6},{6,7},{8,9},{9,10},{10,11},{11... | collective-permute-start | bytes 12296 | tf_op jit(solution)/shard_map/ppermute | solution.py:23
  155.7 6.0 %collective-permute-done.27 = f32[2,8,16,4]{3,2,1,0:T(8,128)S(1)} collective-permute-done((f32[2,8,16,4]{3,2,1,0:T(8,128)S(1)}, f32[2,8,16,4]{3,2,1,0:T(8,128)S(1)}, u32[]{:S(2)}, u32[]{:S(2)}) %collective-permute-start.27) | collective-permute-done | bytes 4128 | tf_op jit(solution)/shard_map/ppermute | solution.py:25
  171.8 7.6 %collective-permute-start.29 = (f32[2,8,1,128]{3,2,1,0:T(1,128)S(1)}, f32[2,8,1,128]{3,2,1,0:T(1,128)S(1)}, u32[]{:S(2)}, u32[]{:S(2)}) collective-permute-start(f32[2,8,1,128]{3,2,1,0:T(1,128)S(1)} %get-tuple-element.306), channel_id=1, source_target_pairs={{0,8},{8,16},{16,24},{24,32},{32,40},{40,48},{48,56},{56,64},{64,7... | collective-permute-start | bytes 24584 | tf_op jit(solution)/shard_map/ppermute | solution.py:23
  181.5 6.7 %collective-permute-start.31 = (f32[2,8,10,1]{3,2,1,0:T(8,128)S(1)}, f32[2,8,10,1]{3,2,1,0:T(8,128)S(1)}, u32[]{:S(2)}, u32[]{:S(2)}) collective-permute-start(f32[2,8,10,1]{3,2,1,0:T(8,128)S(1)} %get-tuple-element.279), channel_id=1, source_target_pairs={{0,1},{1,2},{2,3},{3,4},{4,5},{5,6},{6,7},{8,9},{9,10},{10,11},{11... | collective-permute-start | bytes 1928 | tf_op jit(solution)/shard_map/ppermute | solution.py:23
  190.4 6.7 %collective-permute-start.32 = (f32[2,8,4,128]{3,2,1,0:T(4,128)S(1)}, f32[2,8,4,128]{3,2,1,0:T(4,128)S(1)}, u32[]{:S(2)}, u32[]{:S(2)}) collective-permute-start(f32[2,8,4,128]{3,2,1,0:T(4,128)S(1)} %get-tuple-element.304), channel_id=1, source_target_pairs={{0,8},{8,16},{16,24},{24,32},{32,40},{40,48},{48,56},{56,64},{64,7... | collective-permute-start | bytes 98312 | tf_op jit(solution)/shard_map/ppermute | solution.py:23
  199.0 4.8 %collective-permute-done.33 = f32[2,8,4,128]{3,2,1,0:T(4,128)S(1)} collective-permute-done((f32[2,8,4,128]{3,2,1,0:T(4,128)S(1)}, f32[2,8,4,128]{3,2,1,0:T(4,128)S(1)}, u32[]{:S(2)}, u32[]{:S(2)}) %collective-permute-start.33) | collective-permute-done | bytes 32800 | tf_op jit(solution)/shard_map/ppermute | solution.py:25
  204.0 6.8 %collective-permute-start.34 = (f32[2,8,16,4]{3,2,1,0:T(8,128)S(1)}, f32[2,8,16,4]{3,2,1,0:T(8,128)S(1)}, u32[]{:S(2)}, u32[]{:S(2)}) collective-permute-start(f32[2,8,16,4]{3,2,1,0:T(8,128)S(1)} %get-tuple-element.276), channel_id=1, source_target_pairs={{0,1},{1,2},{2,3},{3,4},{4,5},{5,6},{6,7},{8,9},{9,10},{10,11},{11... | collective-permute-start | bytes 12296 | tf_op jit(solution)/shard_map/ppermute | solution.py:23
  212.7 6.0 %collective-permute-done.35 = f32[2,8,16,4]{3,2,1,0:T(8,128)S(1)} collective-permute-done((f32[2,8,16,4]{3,2,1,0:T(8,128)S(1)}, f32[2,8,16,4]{3,2,1,0:T(8,128)S(1)}, u32[]{:S(2)}, u32[]{:S(2)}) %collective-permute-start.35) | collective-permute-done | bytes 4128 | tf_op jit(solution)/shard_map/ppermute | solution.py:25
  228.8 7.6 %collective-permute-start.37 = (f32[2,8,1,128]{3,2,1,0:T(1,128)S(1)}, f32[2,8,1,128]{3,2,1,0:T(1,128)S(1)}, u32[]{:S(2)}, u32[]{:S(2)}) collective-permute-start(f32[2,8,1,128]{3,2,1,0:T(1,128)S(1)} %get-tuple-element.302), channel_id=1, source_target_pairs={{0,8},{8,16},{16,24},{24,32},{32,40},{40,48},{48,56},{56,64},{64,7... | collective-permute-start | bytes 24584 | tf_op jit(solution)/shard_map/ppermute | solution.py:23
  238.6 6.7 %collective-permute-start.39 = (f32[2,8,10,1]{3,2,1,0:T(8,128)S(1)}, f32[2,8,10,1]{3,2,1,0:T(8,128)S(1)}, u32[]{:S(2)}, u32[]{:S(2)}) collective-permute-start(f32[2,8,10,1]{3,2,1,0:T(8,128)S(1)} %get-tuple-element.275), channel_id=1, source_target_pairs={{0,1},{1,2},{2,3},{3,4},{4,5},{5,6},{6,7},{8,9},{9,10},{10,11},{11... | collective-permute-start | bytes 1928 | tf_op jit(solution)/shard_map/ppermute | solution.py:23
  247.5 6.7 %collective-permute-start.40 = (f32[2,8,4,128]{3,2,1,0:T(4,128)S(1)}, f32[2,8,4,128]{3,2,1,0:T(4,128)S(1)}, u32[]{:S(2)}, u32[]{:S(2)}) collective-permute-start(f32[2,8,4,128]{3,2,1,0:T(4,128)S(1)} %get-tuple-element.300), channel_id=1, source_target_pairs={{0,8},{8,16},{16,24},{24,32},{32,40},{40,48},{48,56},{56,64},{64,7... | collective-permute-start | bytes 98312 | tf_op jit(solution)/shard_map/ppermute | solution.py:23
  261.0 6.8 %collective-permute-start.42 = (f32[2,8,16,4]{3,2,1,0:T(8,128)S(1)}, f32[2,8,16,4]{3,2,1,0:T(8,128)S(1)}, u32[]{:S(2)}, u32[]{:S(2)}) collective-permute-start(f32[2,8,16,4]{3,2,1,0:T(8,128)S(1)} %get-tuple-element.272), channel_id=1, source_target_pairs={{0,1},{1,2},{2,3},{3,4},{4,5},{5,6},{6,7},{8,9},{9,10},{10,11},{11... | collective-permute-start | bytes 12296 | tf_op jit(solution)/shard_map/ppermute | solution.py:23
  269.8 6.0 %collective-permute-done.43 = f32[2,8,16,4]{3,2,1,0:T(8,128)S(1)} collective-permute-done((f32[2,8,16,4]{3,2,1,0:T(8,128)S(1)}, f32[2,8,16,4]{3,2,1,0:T(8,128)S(1)}, u32[]{:S(2)}, u32[]{:S(2)}) %collective-permute-start.43) | collective-permute-done | bytes 4128 | tf_op jit(solution)/shard_map/ppermute | solution.py:25
  285.9 7.6 %collective-permute-start.45 = (f32[2,8,1,128]{3,2,1,0:T(1,128)S(1)}, f32[2,8,1,128]{3,2,1,0:T(1,128)S(1)}, u32[]{:S(2)}, u32[]{:S(2)}) collective-permute-start(f32[2,8,1,128]{3,2,1,0:T(1,128)S(1)} %get-tuple-element.298), channel_id=1, source_target_pairs={{0,8},{8,16},{16,24},{24,32},{32,40},{40,48},{48,56},{56,64},{64,7... | collective-permute-start | bytes 24584 | tf_op jit(solution)/shard_map/ppermute | solution.py:23
  295.7 6.7 %collective-permute-start.47 = (f32[2,8,10,1]{3,2,1,0:T(8,128)S(1)}, f32[2,8,10,1]{3,2,1,0:T(8,128)S(1)}, u32[]{:S(2)}, u32[]{:S(2)}) collective-permute-start(f32[2,8,10,1]{3,2,1,0:T(8,128)S(1)} %get-tuple-element.271), channel_id=1, source_target_pairs={{0,1},{1,2},{2,3},{3,4},{4,5},{5,6},{6,7},{8,9},{9,10},{10,11},{11... | collective-permute-start | bytes 1928 | tf_op jit(solution)/shard_map/ppermute | solution.py:23
  304.5 6.7 %collective-permute-start.48 = (f32[2,8,4,128]{3,2,1,0:T(4,128)S(1)}, f32[2,8,4,128]{3,2,1,0:T(4,128)S(1)}, u32[]{:S(2)}, u32[]{:S(2)}) collective-permute-start(f32[2,8,4,128]{3,2,1,0:T(4,128)S(1)} %get-tuple-element.296), channel_id=1, source_target_pairs={{0,8},{8,16},{16,24},{24,32},{32,40},{40,48},{48,56},{56,64},{64,7... | collective-permute-start | bytes 98312 | tf_op jit(solution)/shard_map/ppermute | solution.py:23
  318.1 6.8 %collective-permute-start.50 = (f32[2,8,16,4]{3,2,1,0:T(8,128)S(1)}, f32[2,8,16,4]{3,2,1,0:T(8,128)S(1)}, u32[]{:S(2)}, u32[]{:S(2)}) collective-permute-start(f32[2,8,16,4]{3,2,1,0:T(8,128)S(1)} %get-tuple-element.268), channel_id=1, source_target_pairs={{0,1},{1,2},{2,3},{3,4},{4,5},{5,6},{6,7},{8,9},{9,10},{10,11},{11... | collective-permute-start | bytes 12296 | tf_op jit(solution)/shard_map/ppermute | solution.py:23
  326.9 6.0 %collective-permute-done.51 = f32[2,8,16,4]{3,2,1,0:T(8,128)S(1)} collective-permute-done((f32[2,8,16,4]{3,2,1,0:T(8,128)S(1)}, f32[2,8,16,4]{3,2,1,0:T(8,128)S(1)}, u32[]{:S(2)}, u32[]{:S(2)}) %collective-permute-start.51) | collective-permute-done | bytes 4128 | tf_op jit(solution)/shard_map/ppermute | solution.py:25
  343.0 7.6 %collective-permute-start.53 = (f32[2,8,1,128]{3,2,1,0:T(1,128)S(1)}, f32[2,8,1,128]{3,2,1,0:T(1,128)S(1)}, u32[]{:S(2)}, u32[]{:S(2)}) collective-permute-start(f32[2,8,1,128]{3,2,1,0:T(1,128)S(1)} %get-tuple-element.294), channel_id=1, source_target_pairs={{0,8},{8,16},{16,24},{24,32},{32,40},{40,48},{48,56},{56,64},{64,7... | collective-permute-start | bytes 24584 | tf_op jit(solution)/shard_map/ppermute | solution.py:23
  352.7 6.7 %collective-permute-start.55 = (f32[2,8,10,1]{3,2,1,0:T(8,128)S(1)}, f32[2,8,10,1]{3,2,1,0:T(8,128)S(1)}, u32[]{:S(2)}, u32[]{:S(2)}) collective-permute-start(f32[2,8,10,1]{3,2,1,0:T(8,128)S(1)} %get-tuple-element.267), channel_id=1, source_target_pairs={{0,1},{1,2},{2,3},{3,4},{4,5},{5,6},{6,7},{8,9},{9,10},{10,11},{11... | collective-permute-start | bytes 1928 | tf_op jit(solution)/shard_map/ppermute | solution.py:23
  362.6 84.9 %all-reduce.237 = f32[256]{0:T(256)S(1)} all-reduce(f32[256]{0:T(256)S(1)} %multiply_dynamic-update-slice_fusion), channel_id=2, replica_groups=mesh['gx'=16,'gy'=8] {'gx','gy'}, use_global_device_ids=true, to_apply=%add.237 | all-reduce | flops 256 | bytes 2048
  (522 shorter events, 162.0 us)
Async XLA Ops:
  1.5 12.8 %collective-permute-start = (f32[2,8,1,128]{3,2,1,0:T(1,128)S(1)}, f32[2,8,1,128]{3,2,1,0:T(1,128)S(1)}, u32[]{:S(2)}, u32[]{:S(2)}) collective-permute-start(f32[2,8,1,128]{3,2,1,0:T(1,128)S(1)} %get-tuple-element.319), channel_id=1, source_target_pairs={{8,0},{16,8},{24,16},{32,24},{40,32},{48,40},{56,48},{64,56},{72,6... | collective-permute-start | bytes 24584 | tf_op jit(solution)/shard_map/ppermute | solution.py:25
  4.8 9.4 %collective-permute-start.1 = (f32[2,8,1,128]{3,2,1,0:T(1,128)S(1)}, f32[2,8,1,128]{3,2,1,0:T(1,128)S(1)}, u32[]{:S(2)}, u32[]{:S(2)}) collective-permute-start(f32[2,8,1,128]{3,2,1,0:T(1,128)S(1)} %get-tuple-element.318), channel_id=1, source_target_pairs={{0,8},{8,16},{16,24},{24,32},{32,40},{40,48},{48,56},{56,64},{64,7... | collective-permute-start | bytes 24584 | tf_op jit(solution)/shard_map/ppermute | solution.py:23
  9.5 27.3 %collective-permute-start.8 = (f32[3,8,4,128]{3,2,1,0:T(4,128)S(1)}, f32[3,8,4,128]{3,2,1,0:T(4,128)S(1)}, u32[]{:S(2)}, u32[]{:S(2)}) collective-permute-start(f32[3,8,4,128]{3,2,1,0:T(4,128)S(1)} %get-tuple-element.292), channel_id=1, source_target_pairs={{0,8},{8,16},{16,24},{24,32},{32,40},{40,48},{48,56},{56,64},{64,7... | collective-permute-start | bytes 147464 | tf_op jit(solution)/shard_map/ppermute | solution.py:23
  11.9 24.9 %collective-permute-start.9 = (f32[3,8,4,128]{3,2,1,0:T(4,128)S(1)}, f32[3,8,4,128]{3,2,1,0:T(4,128)S(1)}, u32[]{:S(2)}, u32[]{:S(2)}) collective-permute-start(f32[3,8,4,128]{3,2,1,0:T(4,128)S(1)} %get-tuple-element.293), channel_id=1, source_target_pairs={{8,0},{16,8},{24,16},{32,24},{40,32},{48,40},{56,48},{64,56},{72,6... | collective-permute-start | bytes 147464 | tf_op jit(solution)/shard_map/ppermute | solution.py:25
  24.2 8.5 %collective-permute-start.4 = (f32[2,8,4,128]{3,2,1,0:T(4,128)S(1)}, f32[2,8,4,128]{3,2,1,0:T(4,128)S(1)}, u32[]{:S(2)}, u32[]{:S(2)}) collective-permute-start(f32[2,8,4,128]{3,2,1,0:T(4,128)S(1)} %get-tuple-element.316), channel_id=1, source_target_pairs={{0,8},{8,16},{16,24},{24,32},{32,40},{40,48},{48,56},{56,64},{64,7... | collective-permute-start | bytes 98312 | tf_op jit(solution)/shard_map/ppermute | solution.py:23
  37.0 11.0 %collective-permute-start.10 = (f32[3,8,16,4]{3,2,1,0:T(8,128)S(1)}, f32[3,8,16,4]{3,2,1,0:T(8,128)S(1)}, u32[]{:S(2)}, u32[]{:S(2)}) collective-permute-start(f32[3,8,16,4]{3,2,1,0:T(8,128)S(1)} %get-tuple-element.264), channel_id=1, source_target_pairs={{0,1},{1,2},{2,3},{3,4},{4,5},{5,6},{6,7},{8,9},{9,10},{10,11},{11... | collective-permute-start | bytes 18440 | tf_op jit(solution)/shard_map/ppermute | solution.py:23
  79.5 8.5 %collective-permute-start.16 = (f32[2,8,4,128]{3,2,1,0:T(4,128)S(1)}, f32[2,8,4,128]{3,2,1,0:T(4,128)S(1)}, u32[]{:S(2)}, u32[]{:S(2)}) collective-permute-start(f32[2,8,4,128]{3,2,1,0:T(4,128)S(1)} %get-tuple-element.312), channel_id=1, source_target_pairs={{0,8},{8,16},{16,24},{24,32},{32,40},{40,48},{48,56},{56,64},{64,7... | collective-permute-start | bytes 98312 | tf_op jit(solution)/shard_map/ppermute | solution.py:23
  124.8 8.3 %collective-permute-start.23 = (f32[2,8,10,1]{3,2,1,0:T(8,128)S(1)}, f32[2,8,10,1]{3,2,1,0:T(8,128)S(1)}, u32[]{:S(2)}, u32[]{:S(2)}) collective-permute-start(f32[2,8,10,1]{3,2,1,0:T(8,128)S(1)} %get-tuple-element.283), channel_id=1, source_target_pairs={{0,1},{1,2},{2,3},{3,4},{4,5},{5,6},{6,7},{8,9},{9,10},{10,11},{11... | collective-permute-start | bytes 1928 | tf_op jit(solution)/shard_map/ppermute | solution.py:23
  133.3 8.6 %collective-permute-start.24 = (f32[2,8,4,128]{3,2,1,0:T(4,128)S(1)}, f32[2,8,4,128]{3,2,1,0:T(4,128)S(1)}, u32[]{:S(2)}, u32[]{:S(2)}) collective-permute-start(f32[2,8,4,128]{3,2,1,0:T(4,128)S(1)} %get-tuple-element.308), channel_id=1, source_target_pairs={{0,8},{8,16},{16,24},{24,32},{32,40},{40,48},{48,56},{56,64},{64,7... | collective-permute-start | bytes 98312 | tf_op jit(solution)/shard_map/ppermute | solution.py:23
  146.9 8.8 %collective-permute-start.26 = (f32[2,8,16,4]{3,2,1,0:T(8,128)S(1)}, f32[2,8,16,4]{3,2,1,0:T(8,128)S(1)}, u32[]{:S(2)}, u32[]{:S(2)}) collective-permute-start(f32[2,8,16,4]{3,2,1,0:T(8,128)S(1)} %get-tuple-element.280), channel_id=1, source_target_pairs={{0,1},{1,2},{2,3},{3,4},{4,5},{5,6},{6,7},{8,9},{9,10},{10,11},{11... | collective-permute-start | bytes 12296 | tf_op jit(solution)/shard_map/ppermute | solution.py:23
  169.8 9.5 %collective-permute-start.28 = (f32[2,8,1,128]{3,2,1,0:T(1,128)S(1)}, f32[2,8,1,128]{3,2,1,0:T(1,128)S(1)}, u32[]{:S(2)}, u32[]{:S(2)}) collective-permute-start(f32[2,8,1,128]{3,2,1,0:T(1,128)S(1)} %get-tuple-element.307), channel_id=1, source_target_pairs={{8,0},{16,8},{24,16},{32,24},{40,32},{48,40},{56,48},{64,56},{72,6... | collective-permute-start | bytes 24584 | tf_op jit(solution)/shard_map/ppermute | solution.py:25
  171.8 8.3 %collective-permute-start.29 = (f32[2,8,1,128]{3,2,1,0:T(1,128)S(1)}, f32[2,8,1,128]{3,2,1,0:T(1,128)S(1)}, u32[]{:S(2)}, u32[]{:S(2)}) collective-permute-start(f32[2,8,1,128]{3,2,1,0:T(1,128)S(1)} %get-tuple-element.306), channel_id=1, source_target_pairs={{0,8},{8,16},{16,24},{24,32},{32,40},{40,48},{48,56},{56,64},{64,7... | collective-permute-start | bytes 24584 | tf_op jit(solution)/shard_map/ppermute | solution.py:23
  180.2 8.4 %collective-permute-start.30 = (f32[2,8,10,1]{3,2,1,0:T(8,128)S(1)}, f32[2,8,10,1]{3,2,1,0:T(8,128)S(1)}, u32[]{:S(2)}, u32[]{:S(2)}) collective-permute-start(f32[2,8,10,1]{3,2,1,0:T(8,128)S(1)} %get-tuple-element.278), channel_id=1, source_target_pairs={{1,0},{2,1},{3,2},{4,3},{5,4},{6,5},{7,6},{9,8},{10,9},{11,10},{12... | collective-permute-start | bytes 1928 | tf_op jit(solution)/shard_map/ppermute | solution.py:25
  181.5 8.6 %collective-permute-start.31 = (f32[2,8,10,1]{3,2,1,0:T(8,128)S(1)}, f32[2,8,10,1]{3,2,1,0:T(8,128)S(1)}, u32[]{:S(2)}, u32[]{:S(2)}) collective-permute-start(f32[2,8,10,1]{3,2,1,0:T(8,128)S(1)} %get-tuple-element.279), channel_id=1, source_target_pairs={{0,1},{1,2},{2,3},{3,4},{4,5},{5,6},{6,7},{8,9},{9,10},{10,11},{11... | collective-permute-start | bytes 1928 | tf_op jit(solution)/shard_map/ppermute | solution.py:23
  190.4 8.6 %collective-permute-start.32 = (f32[2,8,4,128]{3,2,1,0:T(4,128)S(1)}, f32[2,8,4,128]{3,2,1,0:T(4,128)S(1)}, u32[]{:S(2)}, u32[]{:S(2)}) collective-permute-start(f32[2,8,4,128]{3,2,1,0:T(4,128)S(1)} %get-tuple-element.304), channel_id=1, source_target_pairs={{0,8},{8,16},{16,24},{24,32},{32,40},{40,48},{48,56},{56,64},{64,7... | collective-permute-start | bytes 98312 | tf_op jit(solution)/shard_map/ppermute | solution.py:23
  204.0 8.8 %collective-permute-start.34 = (f32[2,8,16,4]{3,2,1,0:T(8,128)S(1)}, f32[2,8,16,4]{3,2,1,0:T(8,128)S(1)}, u32[]{:S(2)}, u32[]{:S(2)}) collective-permute-start(f32[2,8,16,4]{3,2,1,0:T(8,128)S(1)} %get-tuple-element.276), channel_id=1, source_target_pairs={{0,1},{1,2},{2,3},{3,4},{4,5},{5,6},{6,7},{8,9},{9,10},{10,11},{11... | collective-permute-start | bytes 12296 | tf_op jit(solution)/shard_map/ppermute | solution.py:23
  226.9 9.5 %collective-permute-start.36 = (f32[2,8,1,128]{3,2,1,0:T(1,128)S(1)}, f32[2,8,1,128]{3,2,1,0:T(1,128)S(1)}, u32[]{:S(2)}, u32[]{:S(2)}) collective-permute-start(f32[2,8,1,128]{3,2,1,0:T(1,128)S(1)} %get-tuple-element.303), channel_id=1, source_target_pairs={{8,0},{16,8},{24,16},{32,24},{40,32},{48,40},{56,48},{64,56},{72,6... | collective-permute-start | bytes 24584 | tf_op jit(solution)/shard_map/ppermute | solution.py:25
  228.8 8.3 %collective-permute-start.37 = (f32[2,8,1,128]{3,2,1,0:T(1,128)S(1)}, f32[2,8,1,128]{3,2,1,0:T(1,128)S(1)}, u32[]{:S(2)}, u32[]{:S(2)}) collective-permute-start(f32[2,8,1,128]{3,2,1,0:T(1,128)S(1)} %get-tuple-element.302), channel_id=1, source_target_pairs={{0,8},{8,16},{16,24},{24,32},{32,40},{40,48},{48,56},{56,64},{64,7... | collective-permute-start | bytes 24584 | tf_op jit(solution)/shard_map/ppermute | solution.py:23
  237.3 8.4 %collective-permute-start.38 = (f32[2,8,10,1]{3,2,1,0:T(8,128)S(1)}, f32[2,8,10,1]{3,2,1,0:T(8,128)S(1)}, u32[]{:S(2)}, u32[]{:S(2)}) collective-permute-start(f32[2,8,10,1]{3,2,1,0:T(8,128)S(1)} %get-tuple-element.274), channel_id=1, source_target_pairs={{1,0},{2,1},{3,2},{4,3},{5,4},{6,5},{7,6},{9,8},{10,9},{11,10},{12... | collective-permute-start | bytes 1928 | tf_op jit(solution)/shard_map/ppermute | solution.py:25
  238.6 8.6 %collective-permute-start.39 = (f32[2,8,10,1]{3,2,1,0:T(8,128)S(1)}, f32[2,8,10,1]{3,2,1,0:T(8,128)S(1)}, u32[]{:S(2)}, u32[]{:S(2)}) collective-permute-start(f32[2,8,10,1]{3,2,1,0:T(8,128)S(1)} %get-tuple-element.275), channel_id=1, source_target_pairs={{0,1},{1,2},{2,3},{3,4},{4,5},{5,6},{6,7},{8,9},{9,10},{10,11},{11... | collective-permute-start | bytes 1928 | tf_op jit(solution)/shard_map/ppermute | solution.py:23
  247.5 8.6 %collective-permute-start.40 = (f32[2,8,4,128]{3,2,1,0:T(4,128)S(1)}, f32[2,8,4,128]{3,2,1,0:T(4,128)S(1)}, u32[]{:S(2)}, u32[]{:S(2)}) collective-permute-start(f32[2,8,4,128]{3,2,1,0:T(4,128)S(1)} %get-tuple-element.300), channel_id=1, source_target_pairs={{0,8},{8,16},{16,24},{24,32},{32,40},{40,48},{48,56},{56,64},{64,7... | collective-permute-start | bytes 98312 | tf_op jit(solution)/shard_map/ppermute | solution.py:23
  261.0 8.8 %collective-permute-start.42 = (f32[2,8,16,4]{3,2,1,0:T(8,128)S(1)}, f32[2,8,16,4]{3,2,1,0:T(8,128)S(1)}, u32[]{:S(2)}, u32[]{:S(2)}) collective-permute-start(f32[2,8,16,4]{3,2,1,0:T(8,128)S(1)} %get-tuple-element.272), channel_id=1, source_target_pairs={{0,1},{1,2},{2,3},{3,4},{4,5},{5,6},{6,7},{8,9},{9,10},{10,11},{11... | collective-permute-start | bytes 12296 | tf_op jit(solution)/shard_map/ppermute | solution.py:23
  284.0 9.5 %collective-permute-start.44 = (f32[2,8,1,128]{3,2,1,0:T(1,128)S(1)}, f32[2,8,1,128]{3,2,1,0:T(1,128)S(1)}, u32[]{:S(2)}, u32[]{:S(2)}) collective-permute-start(f32[2,8,1,128]{3,2,1,0:T(1,128)S(1)} %get-tuple-element.299), channel_id=1, source_target_pairs={{8,0},{16,8},{24,16},{32,24},{40,32},{48,40},{56,48},{64,56},{72,6... | collective-permute-start | bytes 24584 | tf_op jit(solution)/shard_map/ppermute | solution.py:25
  285.9 8.3 %collective-permute-start.45 = (f32[2,8,1,128]{3,2,1,0:T(1,128)S(1)}, f32[2,8,1,128]{3,2,1,0:T(1,128)S(1)}, u32[]{:S(2)}, u32[]{:S(2)}) collective-permute-start(f32[2,8,1,128]{3,2,1,0:T(1,128)S(1)} %get-tuple-element.298), channel_id=1, source_target_pairs={{0,8},{8,16},{16,24},{24,32},{32,40},{40,48},{48,56},{56,64},{64,7... | collective-permute-start | bytes 24584 | tf_op jit(solution)/shard_map/ppermute | solution.py:23
  294.4 8.4 %collective-permute-start.46 = (f32[2,8,10,1]{3,2,1,0:T(8,128)S(1)}, f32[2,8,10,1]{3,2,1,0:T(8,128)S(1)}, u32[]{:S(2)}, u32[]{:S(2)}) collective-permute-start(f32[2,8,10,1]{3,2,1,0:T(8,128)S(1)} %get-tuple-element.270), channel_id=1, source_target_pairs={{1,0},{2,1},{3,2},{4,3},{5,4},{6,5},{7,6},{9,8},{10,9},{11,10},{12... | collective-permute-start | bytes 1928 | tf_op jit(solution)/shard_map/ppermute | solution.py:25
  295.7 8.6 %collective-permute-start.47 = (f32[2,8,10,1]{3,2,1,0:T(8,128)S(1)}, f32[2,8,10,1]{3,2,1,0:T(8,128)S(1)}, u32[]{:S(2)}, u32[]{:S(2)}) collective-permute-start(f32[2,8,10,1]{3,2,1,0:T(8,128)S(1)} %get-tuple-element.271), channel_id=1, source_target_pairs={{0,1},{1,2},{2,3},{3,4},{4,5},{5,6},{6,7},{8,9},{9,10},{10,11},{11... | collective-permute-start | bytes 1928 | tf_op jit(solution)/shard_map/ppermute | solution.py:23
  304.5 8.6 %collective-permute-start.48 = (f32[2,8,4,128]{3,2,1,0:T(4,128)S(1)}, f32[2,8,4,128]{3,2,1,0:T(4,128)S(1)}, u32[]{:S(2)}, u32[]{:S(2)}) collective-permute-start(f32[2,8,4,128]{3,2,1,0:T(4,128)S(1)} %get-tuple-element.296), channel_id=1, source_target_pairs={{0,8},{8,16},{16,24},{24,32},{32,40},{40,48},{48,56},{56,64},{64,7... | collective-permute-start | bytes 98312 | tf_op jit(solution)/shard_map/ppermute | solution.py:23
  318.1 8.8 %collective-permute-start.50 = (f32[2,8,16,4]{3,2,1,0:T(8,128)S(1)}, f32[2,8,16,4]{3,2,1,0:T(8,128)S(1)}, u32[]{:S(2)}, u32[]{:S(2)}) collective-permute-start(f32[2,8,16,4]{3,2,1,0:T(8,128)S(1)} %get-tuple-element.268), channel_id=1, source_target_pairs={{0,1},{1,2},{2,3},{3,4},{4,5},{5,6},{6,7},{8,9},{9,10},{10,11},{11... | collective-permute-start | bytes 12296 | tf_op jit(solution)/shard_map/ppermute | solution.py:23
  341.0 9.5 %collective-permute-start.52 = (f32[2,8,1,128]{3,2,1,0:T(1,128)S(1)}, f32[2,8,1,128]{3,2,1,0:T(1,128)S(1)}, u32[]{:S(2)}, u32[]{:S(2)}) collective-permute-start(f32[2,8,1,128]{3,2,1,0:T(1,128)S(1)} %get-tuple-element.295), channel_id=1, source_target_pairs={{8,0},{16,8},{24,16},{32,24},{40,32},{48,40},{56,48},{64,56},{72,6... | collective-permute-start | bytes 24584 | tf_op jit(solution)/shard_map/ppermute | solution.py:25
  343.0 8.3 %collective-permute-start.53 = (f32[2,8,1,128]{3,2,1,0:T(1,128)S(1)}, f32[2,8,1,128]{3,2,1,0:T(1,128)S(1)}, u32[]{:S(2)}, u32[]{:S(2)}) collective-permute-start(f32[2,8,1,128]{3,2,1,0:T(1,128)S(1)} %get-tuple-element.294), channel_id=1, source_target_pairs={{0,8},{8,16},{16,24},{24,32},{32,40},{40,48},{48,56},{56,64},{64,7... | collective-permute-start | bytes 24584 | tf_op jit(solution)/shard_map/ppermute | solution.py:23
  351.4 8.4 %collective-permute-start.54 = (f32[2,8,10,1]{3,2,1,0:T(8,128)S(1)}, f32[2,8,10,1]{3,2,1,0:T(8,128)S(1)}, u32[]{:S(2)}, u32[]{:S(2)}) collective-permute-start(f32[2,8,10,1]{3,2,1,0:T(8,128)S(1)} %get-tuple-element.266), channel_id=1, source_target_pairs={{1,0},{2,1},{3,2},{4,3},{5,4},{6,5},{7,6},{9,8},{10,9},{11,10},{12... | collective-permute-start | bytes 1928 | tf_op jit(solution)/shard_map/ppermute | solution.py:25
  352.7 8.6 %collective-permute-start.55 = (f32[2,8,10,1]{3,2,1,0:T(8,128)S(1)}, f32[2,8,10,1]{3,2,1,0:T(8,128)S(1)}, u32[]{:S(2)}, u32[]{:S(2)}) collective-permute-start(f32[2,8,10,1]{3,2,1,0:T(8,128)S(1)} %get-tuple-element.267), channel_id=1, source_target_pairs={{0,1},{1,2},{2,3},{3,4},{4,5},{5,6},{6,7},{8,9},{9,10},{10,11},{11... | collective-permute-start | bytes 1928 | tf_op jit(solution)/shard_map/ppermute | solution.py:23
  (29 other events, 632.3 us)
where the time goes:
time: 458 us; the launch traced here: 449 us
  starting transfers between devices  220 us (48%)
  blocking collectives  84.9 us (19%)
  waiting for transfers between devices  84.4 us (18%)
  other arithmetic  51.1 us (11%)
  between operations  4.78 us (1%)
    ppermute x28, starting transfers between devices, with_halo(): lax.ppermute(tail, axis, [(i, (i + 1) % count) for i in range(ends)])  173 us
    unnamed x1, blocking collectives  84.9 us
    ppermute x28, waiting for transfers between devices, with_halo(): lax.ppermute(head, axis, [((i + 1) % count, i) for i in range(ends)])  67 us
    ppermute x28, starting transfers between devices, with_halo(): lax.ppermute(head, axis, [((i + 1) % count, i) for i in range(ends)])  47.8 us
    add x122, other arithmetic, neighbour_op(): near = near + zpad[:, 2:] + zpad[:, :-2]  24.2 us
    ppermute x28, waiting for transfers between devices, with_halo(): lax.ppermute(tail, axis, [(i, (i + 1) % count) for i in range(ends)])  17.4 us
    mul x114, other arithmetic, local_solve(): correction = (correction + OMEGA * (residual - image) / scale) * inside  13.2 us
    sub x121, other arithmetic, neighbour_op(): first = s11 * centre[0] + s12 * centre[1] + diag * centre[0] - near[0]  10 us
  transfers between devices with their start and end apart: 56, of which 38 were waited for; matrix products, arithmetic and copies ran while one was open for 0% of the time, Pallas kernels for 0%

commit v1 on v0

v1 whole, which is shorter than its diff:
```python
import jax
import jax.numpy as jnp
from jax import lax
from jax.experimental import pallas as pl
from jax.experimental.pallas import tpu as pltpu
from jax.sharding import PartitionSpec as P

SWEEPS = 20
OMEGA = 0.8
PAD = 8
WIN = (16, 13, 10, 7, 4)
KEEP = (104, 80, 56, 32, 8)
ROWS = 400
F32 = jnp.float32
NGX = 16
NGY = 8


def iota(shape, dim):
    return lax.broadcasted_iota(jnp.int32, shape, dim)


def roll(x, by, axis):
    by = by % x.shape[axis]
    return x if by == 0 else pltpu.roll(x, by, axis)


def lane_ids():
    lane = iota((8, 128), 1)
    return lane & 15, lane >> 4


def edge_columns(tiles):
    lane = iota((8, 128), 1)
    out = jnp.zeros((8, 128), F32)
    for n, tile in enumerate(tiles):
        out = jnp.where(lane == n, roll(tile, n, 1), out)
        out = jnp.where(lane == 16 + n, roll(tile, 17 + n, 1), out)
    return out


def pack_kernel(mix, forc, lab, basis, colour, out):
    for f in range(3):
        out[f * 8 : f * 8 + 8] = mix[f]
    for f in range(2):
        out[24 + f * 8 : 32 + f * 8] = forc[f]
    out[40:48] = lab[...].astype(F32)
    cols = edge_columns([basis[f, z] for f in range(2) for z in range(8)])
    lane = iota((8, 128), 1)
    out[48] = jnp.where(lane == 32, colour[0, 0].astype(F32), cols)


def rows_kernel(own, left, right, basis, up, down):
    for part, ref in enumerate((left, own, right)):
        lanes = slice(part * 128, part * 128 + 128)
        for a in range(6):
            for p in range(4):
                lo, hi = ref[a * 8 + 2 * p], ref[a * 8 + 2 * p + 1]
                sub = iota((8, 128), 0)
                up[a * 4 + p, :, lanes] = jnp.where(sub < 4, lo, roll(hi, 4, 0))
                down[a * 4 + p, :, lanes] = jnp.where(sub < 4, roll(lo, 4, 0), hi)
        for z in range(8):
            up[24, z : z + 1, lanes] = ref[40 + z, 4:5, :]
            down[24, z : z + 1, lanes] = ref[40 + z, 3:4, :]
            for f in range(2):
                if part == 1:
                    up[25 + f, z : z + 1, lanes] = basis[f, z, 0:1, :]
                    down[25 + f, z : z + 1, lanes] = basis[f, z, 7:8, :]
        if part != 1:
            up[25:27, :, lanes] = jnp.zeros((2, 8, 128), F32)
            down[25:27, :, lanes] = jnp.zeros((2, 8, 128), F32)


def window_rows(kind, tiles):
    if kind == 0:
        return PAD + 128 - 4
    if kind == 1:
        return PAD + 128 + 4 - 8 * tiles
    return PAD + 128 + 124


def prepare(kind, tiles, stat, u, uo, coef, i, j):
    row0 = window_rows(kind, tiles)
    xp, z = lane_ids()
    sub = iota((8, 128), 0)
    rim_x = ((xp == 0) | (xp == 15)).astype(F32)
    gx = i * 8 + xp - 4
    in_x = ((gx >= 0) & (gx < NGX * 8)).astype(F32)
    for t in range(tiles):
        at = pl.ds(row0 + t, 8, stride=tiles)
        s11, s22, s12 = stat[0, at, :], stat[1, at, :], stat[2, at, :]
        y = row0 - PAD - 128 + sub * tiles + t + j * 128
        inside = in_x * ((y >= 0) & (y < NGY * 128)).astype(F32)
        diag = 6.0 + rim_x
        if t == 0 and kind != 1:
            diag = diag + (sub == 0).astype(F32)
        if t == tiles - 1 and kind != 2:
            diag = diag + (sub == 7).astype(F32)
        vals = []
        for f in range(2):
            c = u[f, at, :]
            near = u[f, pl.ds(row0 + t - 1, 8, stride=tiles), :] + u[f, pl.ds(row0 + t + 1, 8, stride=tiles), :]
            out = uo[f, at, :]
            near = near + jnp.where(xp == 0, out, roll(c, 1, 1)) + jnp.where(xp == 15, out, roll(c, -1, 1))
            near = near + jnp.where(z == 0, 0.0, roll(c, 16, 1)) + jnp.where(z == 7, 0.0, roll(c, -16, 1))
            vals.append((c, near))
        for f, s in ((0, s11), (1, s22)):
            c, near = vals[f]
            r = stat[3 + f, at, :] - ((s + 6.0) * c + s12 * vals[1 - f][0] - near)
            w = OMEGA * inside / (s + diag)
            coef[f, t] = w
            coef[2 + f, t] = w * s12
            coef[4 + f, t] = w * r
            coef[6 + f, t] = w * r


def sweeps(kind, tiles, u, coef):
    row0 = window_rows(kind, tiles)
    xp, z = lane_ids()
    sub = iota((8, 128), 0)

    def body(_, carry):
        firsts, prevs = [], []
        for f in range(2):
            first = coef[6 + f, 0]
            firsts.append(jnp.where(sub == 7, 0.0, roll(first, -1, 0)))
            prevs.append(jnp.where(sub == 0, 0.0, roll(coef[6 + f, tiles - 1], 1, 0)))
        cur = [coef[6, 0], coef[7, 0]]
        for t in range(tiles):
            nxt = [coef[6, t + 1], coef[7, t + 1]] if t + 1 < tiles else firsts
            for f in range(2):
                c = cur[f]
                near = prevs[f] + nxt[f]
                near = near + (jnp.where(xp == 0, 0.0, roll(c, 1, 1)) + jnp.where(xp == 15, 0.0, roll(c, -1, 1)))
                near = near + (jnp.where(z == 0, 0.0, roll(c, 16, 1)) + jnp.where(z == 7, 0.0, roll(c, -16, 1)))
                new = (1.0 - OMEGA) * c + coef[4 + f, t] + (coef[f, t] * near - coef[2 + f, t] * cur[1 - f])
                coef[6 + f, t] = new
            prevs, cur = cur, nxt
        return carry

    lax.fori_loop(0, SWEEPS - 1, body, 0)
    own_x = (xp >= 4) & (xp < 12)
    for t in range(tiles):
        at = pl.ds(row0 + t, 8, stride=tiles)
        y = row0 - PAD - 128 + sub * tiles + t
        if kind == 0:
            here = own_x & (y >= 0) & (y < 128)
        elif kind == 1:
            here = own_x & (y < 0)
        else:
            here = own_x & (y >= 128)
        for f in range(2):
            u[f, at, :] = u[f, at, :] + jnp.where(here, coef[6 + f, t], 0.0)


def solve_round(rnd, stat, u, uo, meta, coefs, i, j):
    own = jnp.max(meta[0:8, :])
    left = jnp.max(meta[8:16, :])
    right = jnp.max(meta[16:24, :])
    jobs = [(0, 17, own, coefs[0])]
    if rnd < 5:
        jobs += [(1, WIN[rnd], left, coefs[1]), (2, WIN[rnd], right, coefs[2])]
    for kind, tiles, colour, coef in jobs:
        pl.when(colour == float(rnd))(lambda kind=kind, tiles=tiles, coef=coef: prepare(kind, tiles, stat, u, uo, coef, i, j))
    for kind, tiles, colour, coef in jobs:
        pl.when(colour == float(rnd))(lambda kind=kind, tiles=tiles, coef=coef: sweeps(kind, tiles, u, coef))


def emit(rnd, u, up, down):
    keep = KEEP[rnd]
    xp, _ = lane_ids()
    for q in range((128 + 2 * keep) // 8):
        src = pl.ds(PAD + 128 - keep + 8 * q, 8)
        a, b = u[0, src, :], u[1, src, :]
        up[pl.ds(8 * q, 8), :] = jnp.where(xp < 5, roll(a, -4, 1), roll(b, 1, 1))
        down[pl.ds(8 * q, 8), :] = jnp.where(xp < 5, roll(a, -7, 1), roll(b, -2, 1))


def absorb(rnd, u, uo, above, below, i):
    keep = KEEP[rnd]
    xp, _ = lane_ids()
    has_above = (i > 0).astype(F32)
    has_below = (i < NGX - 1).astype(F32)
    for q in range((128 + 2 * keep) // 8):
        at = pl.ds(PAD + 128 - keep + 8 * q, 8)
        a = above[pl.ds(8 * q, 8), :] * has_above
        b = below[pl.ds(8 * q, 8), :] * has_below
        u[0, at, :] = jnp.where(xp < 4, roll(a, -1, 1), jnp.where(xp >= 12, roll(b, 12, 1), u[0, at, :]))
        u[1, at, :] = jnp.where(xp < 4, roll(a, -6, 1), jnp.where(xp >= 12, roll(b, 7, 1), u[1, at, :]))
        uo[0, at, :] = jnp.where(xp == 0, a, roll(b, 11, 1))
        uo[1, at, :] = jnp.where(xp == 0, roll(a, -5, 1), roll(b, 6, 1))


def start_kernel(own, left, right, above, below, stat, u, meta, fin, up, down, buf, uo, c0, c1, c2):
    i = lax.axis_index("gx")
    j = lax.axis_index("gy")
    xp, _ = lane_ids()
    lane = iota((8, 128), 1)
    full_lane = iota((128, 128), 1)
    full_xp = full_lane & 15
    gx = i * 8 + full_xp - 4
    in_x = (gx >= 0) & (gx < NGX * 8)
    for n, ref in enumerate((own, left, right)):
        valid = ((j > 0) if n == 1 else (j < NGY - 1)) if n else (j >= 0)
        colour = jnp.where(lane == 32, jnp.where(valid, 1.0, 0.0) * (ref[48] + 1.0), 0.0) - 1.0
        meta[n * 8 : n * 8 + 8, :] = colour
    fin[0] = left[48] * (j > 0).astype(F32)
    fin[1] = right[48] * (j < NGY - 1).astype(F32)
    for f in range(2):
        fin[2 + f] = above[25 + f, :, 128:256] * (i > 0).astype(F32)
        fin[4 + f] = below[25 + f, :, 128:256] * (i < NGX - 1).astype(F32)
    for f in range(2):
        u[f, 0:PAD, :] = jnp.zeros((PAD, 128), F32)
        u[f, ROWS - PAD : ROWS, :] = jnp.zeros((PAD, 128), F32)
    for part, ref in enumerate((left, own, right)):
        lanes = slice(part * 128, part * 128 + 128)
        rows = slice(PAD + part * 128, PAD + part * 128 + 128)
        gy = (j - 1 + part) * 128
        in_y = (gy >= 0) & (gy < NGY * 128)

        def gather(a):
            slot = a % 2
            for p in range(4):
                for h in range(2):
                    z = 2 * p + h
                    buf[slot, z * 16 : z * 16 + 4, :] = above[a * 4 + p, 4 * h : 4 * h + 4, lanes]
                    buf[slot, z * 16 + 4 : z * 16 + 12, :] = ref[a * 8 + z]
                    buf[slot, z * 16 + 12 : z * 16 + 16, :] = below[a * 4 + p, 4 * h : 4 * h + 4, lanes]
            return buf[slot].T

        stat[0, rows, :] = gather(0)
        stat[1, rows, :] = gather(1)
        stat[2, rows, :] = 0.25 * (gather(2) - 0.125)
        force = [gather(3), gather(4)]
        label = gather(5)
        buf[0] = jnp.zeros((128, 128), F32)
        for z in range(8):
            buf[0, z * 16 : z * 16 + 1, :] = above[24, z : z + 1, lanes]
            buf[0, z * 16 + 15 : z * 16 + 16, :] = below[24, z : z + 1, lanes]
        outer = buf[0].T
        y_ok = in_y.astype(F32)
        out_ok = jnp.where(full_xp == 0, (i > 0).astype(F32), (i < NGX - 1).astype(F32)) * y_ok
        for f in range(2):
            hot = (label == f + 1.0).astype(F32) * (in_x.astype(F32) * y_ok)
            u[f, rows, :] = hot
            stat[3 + f, rows, :] = hot + force[f]
            uo[f, rows, :] = (outer == f + 1.0).astype(F32) * out_ok
    solve_round(0, stat, u, uo, meta, (c0, c1, c2), i, j)
    emit(0, u, up, down)


def middle_kernel(rnd, stat, u_in, meta, above, below, u, up, down, uo, c0, c1, c2):
    i = lax.axis_index("gx")
    j = lax.axis_index("gy")
    u[...] = u_in[...]
    absorb(rnd - 1, u, uo, above, below, i)
    solve_round(rnd, stat, u, uo, meta, (c0, c1, c2), i, j)
    emit(rnd, u, up, down)


def last_kernel(stat, u_in, meta, above, below, fin, mix, forc, lab, basis, nat, send, u, uo, c0):
    i = lax.axis_index("gx")
    j = lax.axis_index("gy")
    u[...] = u_in[...]
    absorb(4, u, uo, above, below, i)
    solve_round(5, stat, u, uo, meta, (c0,), i, j)
    sub = iota((8, 128), 0)
    lane = iota((8, 128), 1)
    tiles = []
    for f in range(2):
        flat = u[f, PAD + 128 : PAD + 256, :].T
        for z in range(8):
            tile = flat[z * 16 + 4 : z * 16 + 12, :]
            nat[f, z] = tile
            tiles.append(tile)
    cols = edge_columns(tiles)
    sums = [jnp.zeros((8, 128), F32) for _ in range(10)]
    left = cols * roll(fin[0], -16, 1)
    right = cols * roll(fin[1], 16, 1)
    for f in range(2):
        acc = jnp.zeros((8, 128), F32)
        for z in range(8):
            c, other = tiles[f * 8 + z], tiles[(1 - f) * 8 + z]
            near = jnp.where(sub == 0, 0.0, roll(c, 1, 0)) + jnp.where(sub == 7, 0.0, roll(c, -1, 0))
            near = near + jnp.where(lane == 0, 0.0, roll(c, 1, 1)) + jnp.where(lane == 127, 0.0, roll(c, -1, 1))
            if z > 0:
                near = near + tiles[f * 8 + z - 1]
            if z < 7:
                near = near + tiles[f * 8 + z + 1]
            s12 = 0.25 * (mix[2, z] - 0.125)
            rhs = (lab[z] == f + 1).astype(F32) + forc[f, z]
            acc = acc + basis[f, z] * (rhs - ((mix[f, z] + 6.0) * c + s12 * other - near))
        sums[f] = acc
        top = jnp.zeros((8, 128), F32)
        bot = jnp.zeros((8, 128), F32)
        for z in range(8):
            top = jnp.where(sub == z, jnp.broadcast_to(tiles[f * 8 + z][0:1, :], (8, 128)), top)
            bot = jnp.where(sub == z, jnp.broadcast_to(tiles[f * 8 + z][7:8, :], (8, 128)), bot)
        sums[2 + f] = top * fin[2 + f]
        sums[4 + f] = bot * fin[4 + f]
        sums[6 + f] = jnp.where((lane >= f * 8) & (lane < f * 8 + 8), left, 0.0)
        sums[8 + f] = jnp.where((lane >= 16 + f * 8) & (lane < 24 + f * 8), right, 0.0)
    here = i * NGY + j
    slot = iota((2, 128), 0) * 128 + iota((2, 128), 1)
    row = jnp.zeros((2, 128), F32)
    for n, at in enumerate((here, here - NGY, here + NGY, here - 1, here + 1)):
        for f in range(2):
            total = jnp.sum(sums[2 * n + f], keepdims=True) * (1.0 / 8192.0)
            row = jnp.where(slot == 2 * at + f, total, row)
    send[...] = jnp.broadcast_to(row[None], (NGX * NGY, 2, 128))


def lift_kernel(got, inv, basis, nat, out, coarse):
    q = jnp.sum(got[...], axis=0)
    lane = iota((1, 2), 1)
    pair = jnp.zeros((1, 2), F32)
    for f in range(2):
        c = jnp.sum(q[0:1, :] * inv[0, 0, f : f + 1, 0:128] + q[1:2, :] * inv[0, 0, f : f + 1, 128:256], keepdims=True)
        out[f] = nat[f] + basis[f] * c.reshape(1, 1, 1)
        pair = jnp.where(lane == f, c, pair)
    coarse[0] = pair


def sds(*shape):
    return jax.ShapeDtypeStruct(shape, F32)


def call(kernel, out, scratch=(), **kw):
    vm = pl.BlockSpec(memory_space=pltpu.VMEM)
    return pl.pallas_call(
        kernel,
        out_shape=out,
        scratch_shapes=list(scratch),
        compiler_params=pltpu.CompilerParams(vmem_limit_bytes=48 * 1024 * 1024),
        **kw,
    )


def shift(x, axis, by):
    n = lax.axis_size(axis)
    return lax.ppermute(x, axis, [(k, (k + by) % n) for k in range(n)])


def shards(mixing, forcing, labels, colours, coarse_basis, coarse_inverse):
    vm = pl.BlockSpec(memory_space=pltpu.VMEM)
    coef = lambda t: pltpu.VMEM((8, t, 8, 128), F32)
    block = call(
        pack_kernel, sds(49, 8, 128), in_specs=[vm] * 4 + [pl.BlockSpec(memory_space=pltpu.SMEM)], name="pack"
    )(mixing, forcing, labels, coarse_basis, colours)
    left = shift(block, "gy", 1)
    right = shift(block, "gy", -1)
    up, down = call(rows_kernel, (sds(27, 8, 384), sds(27, 8, 384)), name="rows")(block, left, right, coarse_basis)
    above = shift(down, "gx", 1)
    below = shift(up, "gx", -1)
    msg = lambda r: sds(128 + 2 * KEEP[r], 128)
    stat, u, meta, fin, up, down = call(
        start_kernel,
        (sds(5, ROWS, 128), sds(2, ROWS, 128), sds(24, 128), sds(6, 8, 128), msg(0), msg(0)),
        [pltpu.VMEM((2, 128, 128), F32), pltpu.VMEM((2, ROWS, 128), F32), coef(17), coef(16), coef(16)],
        name="round0",
    )(block, left, right, above, below)
    for rnd in range(1, 5):
        above = shift(down, "gx", 1)
        below = shift(up, "gx", -1)
        u, up, down = call(
            lambda *refs, rnd=rnd: middle_kernel(rnd, *refs),
            (sds(2, ROWS, 128), msg(rnd), msg(rnd)),
            [pltpu.VMEM((2, ROWS, 128), F32), coef(17), coef(16), coef(16)],
            name=f"round{rnd}",
        )(stat, u, meta, above, below)
    above = shift(down, "gx", 1)
    below = shift(up, "gx", -1)
    nat, send = call(
        last_kernel,
        (sds(2, 8, 8, 128), sds(NGX * NGY, 2, 128)),
        [pltpu.VMEM((2, ROWS, 128), F32), pltpu.VMEM((2, ROWS, 128), F32), coef(17)],
        name="round5",
    )(stat, u, meta, above, below, fin, mixing, forcing, labels, coarse_basis)
    got = lax.all_to_all(send, ("gx", "gy"), 0, 0, tiled=True)
    return call(lift_kernel, (sds(2, 8, 8, 128), sds(1, 1, 2)), name="lift")(got, coarse_inverse, coarse_basis, nat)


def solution(mesh):
    return jax.shard_map(
        shards,
        mesh=mesh,
        in_specs=(
            P(None, None, "gx", "gy"),
            P(None, None, "gx", "gy"),
            P(None, "gx", "gy"),
            P("gx", "gy"),
            P(None, None, "gx", "gy"),
            P("gx", "gy", None, None),
        ),
        out_specs=(P(None, None, "gx", "gy"), P("gx", "gy", None)),
        check_vma=False,
    )
```

time: 458 us -> 112 us (0.24); the launches traced: 449 us -> 112 us
  starting transfers between devices: 220 us -> 17.5 us
  blocking collectives: 84.9 us -> 28.9 us
  other arithmetic: 51.1 us -> 0 us
  waiting for transfers between devices: 84.4 us -> 50.1 us
  Pallas kernels: 0 us -> 11.2 us
    ppermute x56 -> x14, starting transfers between devices: 220 us -> 17.5 us  [shift(): return lax.ppermute(x, axis, [(k, (k + by) % n) for k in range(n)])]
    unnamed x1 -> x0, blocking collectives: 84.9 us -> none
    ppermute x56 -> x14, waiting for transfers between devices: 84.4 us -> 50.1 us  [shift(): return lax.ppermute(x, axis, [(k, (k + by) % n) for k in range(n)])]
    all_to_all x0 -> x1, blocking collectives: none -> 28.9 us  [shards(): got = lax.all_to_all(send, ('gx', 'gy'), 0, 0, tiled=True)]
    add x134 -> x0, other arithmetic: 26 us -> none  [the longest x122 24.2 us: neighbour_op(): near = near + zpad[:, 2:] + zpad[:, :-2]]
    mul x114 -> x0, other arithmetic: 13.2 us -> none  [local_solve(): correction = (correction + OMEGA * (residual - image) / scale) * inside]
    pallas_call x0 -> x9, Pallas kernels: none -> 11.2 us  [the longest x4 8.74 us: shards(): call(lambda *refs, rnd=rnd: middle_kernel(rnd, *refs), (sds(2, ROWS, 128)...]
    sub x127 -> x0, other arithmetic: 10.1 us -> none  [the longest x121 10 us: neighbour_op(): first = s11 * centre[0] + s12 * centre[1] + diag * centre[0] - near[0]]
  transfers between devices with their start and end apart: 56 -> 14, of which waited for: 38 -> 14; matrix products, arithmetic and copies ran while one was open for 0% -> 0% of each run, Pallas kernels for 0% -> 0%
where the time goes in v1:
time: 112 us
  waiting for transfers between devices  50.1 us (45%)
  blocking collectives  28.9 us (26%)
  starting transfers between devices  17.5 us (16%)
  Pallas kernels  11.2 us (10%)
  local copies, waits for them, and re-layouts  3.34 us (3%)
  between operations  1.42 us (1%)
    ppermute x14, waiting for transfers between devices, shift(): return lax.ppermute(x, axis, [(k, (k + by) % n) for k in range(n)])  50.1 us
    all_to_all x1, blocking collectives, shards(): got = lax.all_to_all(send, ('gx', 'gy'), 0, 0, tiled=True)  28.9 us
    ppermute x14, starting transfers between devices, shift(): return lax.ppermute(x, axis, [(k, (k + by) % n) for k in range(n)])  17.5 us
    pallas_call x4, Pallas kernels, shards(): call(lambda *refs, rnd=rnd: middle_kernel(rnd, *refs), (sds(2, ROWS, 128)...  8.74 us
    unnamed x18, local copies, waits for them, and re-layouts  3.34 us
  transfers between devices with their start and end apart: 14, of which 14 were waited for; matrix products, arithmetic and copies ran while one was open for 0% of the time, Pallas kernels for 0%

profile of v1, /device:TPU:1, one launch (start us, length us, event | category | flops | bytes accessed | tf_op | source)
XLA Modules:
  0.0 112.4 jit_solution(4476342563620912181)
XLA Ops:
  1.3 0.8 copy-done
  2.1 0.9 copy-done.2
  3.0 0.8 copy-done.4
  3.9 0.8 copy-done.6
  4.7 5.6 %collective-permute-start.1 = (f32[49,8,128]{2,1,0:T(8,128)S(1)}, f32[49,8,128]{2,1,0:T(8,128)S(1)}, u32[]{:S(2)}, u32[]{:S(2)}) collective-permute-start(f32[49,8,128]{2,1,0:T(8,128)S(1)} %pack.1.own), channel_id=1, source_target_pairs={{0,7},{1,0},{2,1},{3,2},{4,3},{5,4},{6,5},{7,6},{8,15},{9,8},{10,9... | collective-permute-start | bytes 602120 | tf_op jit(solution)/shard_map/ppermute | solution.py:341
  10.3 3.7 %collective-permute-done.1.right = f32[49,8,128]{2,1,0:T(8,128)S(1)} collective-permute-done((f32[49,8,128]{2,1,0:T(8,128)S(1)}, f32[49,8,128]{2,1,0:T(8,128)S(1)}, u32[]{:S(2)}, u32[]{:S(2)}) %collective-permute-start.1) | collective-permute-done | bytes 200736 | tf_op jit(solution)/shard_map/ppermute | solution.py:341
  14.0 4.0 %collective-permute-done.left = f32[49,8,128]{2,1,0:T(8,128)S(1)} collective-permute-done((f32[49,8,128]{2,1,0:T(8,128)S(1)}, f32[49,8,128]{2,1,0:T(8,128)S(1)}, u32[]{:S(2)}, u32[]{:S(2)}) %collective-permute-start) | collective-permute-done | bytes 200736 | tf_op jit(solution)/shard_map/ppermute | solution.py:341
  18.0 4.3 %collective-permute-start.2 = (f32[27,8,384]{2,1,0:T(8,128)S(1)}, f32[27,8,384]{2,1,0:T(8,128)S(1)}, u32[]{:S(2)}, u32[]{:S(2)}) collective-permute-start(f32[27,8,384]{2,1,0:T(8,128)S(1)} %get-tuple-element.24), channel_id=1, source_target_pairs={{0,8},{8,16},{16,24},{24,32},{32,40},{40,48},{48,56},{56,64},{64,7... | collective-permute-start | bytes 995336 | tf_op jit(solution)/shard_map/ppermute | solution.py:341
  22.3 4.3 %collective-permute-done.2.above = f32[27,8,384]{2,1,0:T(8,128)S(1)} collective-permute-done((f32[27,8,384]{2,1,0:T(8,128)S(1)}, f32[27,8,384]{2,1,0:T(8,128)S(1)}, u32[]{:S(2)}, u32[]{:S(2)}) %collective-permute-start.2) | collective-permute-done | bytes 331808 | tf_op jit(solution)/shard_map/ppermute | solution.py:341
  26.6 5.2 %collective-permute-done.3.below = f32[27,8,384]{2,1,0:T(8,128)S(1)} collective-permute-done((f32[27,8,384]{2,1,0:T(8,128)S(1)}, f32[27,8,384]{2,1,0:T(8,128)S(1)}, u32[]{:S(2)}, u32[]{:S(2)}) %collective-permute-start.3) | collective-permute-done | bytes 331808 | tf_op jit(solution)/shard_map/ppermute | solution.py:341
  31.9 0.8 round0.1
  32.8 0.5 collective-permute-start.5
  33.3 1.8 %collective-permute-done.4.refs_3_ = f32[336,128]{1,0:T(8,128)S(1)} collective-permute-done((f32[336,128]{1,0:T(8,128)S(1)}, f32[336,128]{1,0:T(8,128)S(1)}, u32[]{:S(2)}, u32[]{:S(2)}) %collective-permute-start.4) | collective-permute-done | bytes 172064 | tf_op jit(solution)/shard_map/ppermute | solution.py:341
  35.1 4.1 %collective-permute-done.5.refs_4_ = f32[336,128]{1,0:T(8,128)S(1)} collective-permute-done((f32[336,128]{1,0:T(8,128)S(1)}, f32[336,128]{1,0:T(8,128)S(1)}, u32[]{:S(2)}, u32[]{:S(2)}) %collective-permute-start.5) | collective-permute-done | bytes 172064 | tf_op jit(solution)/shard_map/ppermute | solution.py:341
  39.2 0.7 round1.1
  39.8 5.3 %collective-permute-start.6 = (f32[288,128]{1,0:T(8,128)S(1)}, f32[288,128]{1,0:T(8,128)S(1)}, u32[]{:S(2)}, u32[]{:S(2)}) collective-permute-start(f32[288,128]{1,0:T(8,128)S(1)} %get-tuple-element.32), channel_id=1, source_target_pairs={{0,8},{8,16},{16,24},{24,32},{32,40},{40,48},{48,56},{56,64},{64,7... | collective-permute-start | bytes 442376 | tf_op jit(solution)/shard_map/ppermute | solution.py:341
  45.1 2.1 %collective-permute-done.6.refs_3_ = f32[288,128]{1,0:T(8,128)S(1)} collective-permute-done((f32[288,128]{1,0:T(8,128)S(1)}, f32[288,128]{1,0:T(8,128)S(1)}, u32[]{:S(2)}, u32[]{:S(2)}) %collective-permute-start.6) | collective-permute-done | bytes 147488 | tf_op jit(solution)/shard_map/ppermute | solution.py:341
  47.2 5.5 %collective-permute-done.7.refs_4_ = f32[288,128]{1,0:T(8,128)S(1)} collective-permute-done((f32[288,128]{1,0:T(8,128)S(1)}, f32[288,128]{1,0:T(8,128)S(1)}, u32[]{:S(2)}, u32[]{:S(2)}) %collective-permute-start.7) | collective-permute-done | bytes 147488 | tf_op jit(solution)/shard_map/ppermute | solution.py:341
  52.8 0.6 round2.1
  53.4 0.5 collective-permute-start.9
  53.9 1.4 %collective-permute-done.8.refs_3_ = f32[240,128]{1,0:T(8,128)S(1)} collective-permute-done((f32[240,128]{1,0:T(8,128)S(1)}, f32[240,128]{1,0:T(8,128)S(1)}, u32[]{:S(2)}, u32[]{:S(2)}) %collective-permute-start.8) | collective-permute-done | bytes 122912 | tf_op jit(solution)/shard_map/ppermute | solution.py:341
  55.3 5.5 %collective-permute-done.9.refs_4_ = f32[240,128]{1,0:T(8,128)S(1)} collective-permute-done((f32[240,128]{1,0:T(8,128)S(1)}, f32[240,128]{1,0:T(8,128)S(1)}, u32[]{:S(2)}, u32[]{:S(2)}) %collective-permute-start.9) | collective-permute-done | bytes 122912 | tf_op jit(solution)/shard_map/ppermute | solution.py:341
  60.8 4.9 %round3.1 = (f32[2,400,128]{2,1,0:T(8,128)S(1)}, f32[192,128]{1,0:T(8,128)S(1)}, f32[192,128]{1,0:T(8,128)S(1)}) custom-call(f32[5,400,128]{2,1,0:T(8,128)S(1)} %get-tuple-element.26.refs_0_.stat, f32[2,400,128]{2,1,0:T(8,128)S(1)} %get-tuple-element.34.refs_1_, f32[24,128]{1,0:T(8,128)S(1)} %get-tuple-element.28.refs_2_.meta, ...), custom_call_target="tpu_custom_call" | custom-call | tf_op jit(solution)/shard_map/round3/pallas_call | solution.py:365
  66.3 1.1 %collective-permute-done.10.refs_3_ = f32[192,128]{1,0:T(8,128)S(1)} collective-permute-done((f32[192,128]{1,0:T(8,128)S(1)}, f32[192,128]{1,0:T(8,128)S(1)}, u32[]{:S(2)}, u32[]{:S(2)}) %collective-permute-start.10) | collective-permute-done | bytes 98336 | tf_op jit(solution)/shard_map/ppermute | solution.py:341
  67.4 4.9 %collective-permute-done.11.refs_4_ = f32[192,128]{1,0:T(8,128)S(1)} collective-permute-done((f32[192,128]{1,0:T(8,128)S(1)}, f32[192,128]{1,0:T(8,128)S(1)}, u32[]{:S(2)}, u32[]{:S(2)}) %collective-permute-start.11) | collective-permute-done | bytes 98336 | tf_op jit(solution)/shard_map/ppermute | solution.py:341
  72.4 2.6 %round4.1 = (f32[2,400,128]{2,1,0:T(8,128)S(1)}, f32[144,128]{1,0:T(8,128)S(1)}, f32[144,128]{1,0:T(8,128)S(1)}) custom-call(f32[5,400,128]{2,1,0:T(8,128)S(1)} %get-tuple-element.26.refs_0_.stat, f32[2,400,128]{2,1,0:T(8,128)S(1)} %get-tuple-element.37.refs_1_, f32[24,128]{1,0:T(8,128)S(1)} %get-tuple-element.28.refs_2_.meta, ...), custom_call_target="tpu_custom_call" | custom-call | tf_op jit(solution)/shard_map/round4/pallas_call | solution.py:365
  75.1 0.5 collective-permute-start.13
  75.6 0.9 collective-permute-done.12.above
  76.5 5.5 %collective-permute-done.13.below = f32[144,128]{1,0:T(8,128)S(1)} collective-permute-done((f32[144,128]{1,0:T(8,128)S(1)}, f32[144,128]{1,0:T(8,128)S(1)}, u32[]{:S(2)}, u32[]{:S(2)}) %collective-permute-start.13) | collective-permute-done | bytes 73760 | tf_op jit(solution)/shard_map/ppermute | solution.py:341
  82.0 0.6 round5.1
  82.7 28.9 %all_to_all.5.got = f32[128,2,128]{2,1,0:T(2,128)S(1)} all-to-all(f32[128,2,128]{2,1,0:T(2,128)S(1)} %get-tuple-element.44), channel_id=1, replica_groups=mesh['gx'=16,'gy'=8] {'gx','gy'}, dimensions={0} | all-to-all | bytes 262144 | tf_op jit(solution)/shard_map/all_to_all | solution.py:379
  111.5 0.9 lift.1
  (24 shorter events, 1.0 us)
Async XLA Ops:
  1.3 0.8 copy-start
  2.1 0.9 copy-start.2
  3.0 0.8 copy-start.4
  3.9 0.8 copy-start.6
  4.7 9.2 %collective-permute-start.1 = (f32[49,8,128]{2,1,0:T(8,128)S(1)}, f32[49,8,128]{2,1,0:T(8,128)S(1)}, u32[]{:S(2)}, u32[]{:S(2)}) collective-permute-start(f32[49,8,128]{2,1,0:T(8,128)S(1)} %pack.1.own), channel_id=1, source_target_pairs={{0,7},{1,0},{2,1},{3,2},{4,3},{5,4},{6,5},{7,6},{8,15},{9,8},{10,9... | collective-permute-start | bytes 602120 | tf_op jit(solution)/shard_map/ppermute | solution.py:341
  10.3 7.6 %collective-permute-start = (f32[49,8,128]{2,1,0:T(8,128)S(1)}, f32[49,8,128]{2,1,0:T(8,128)S(1)}, u32[]{:S(2)}, u32[]{:S(2)}) collective-permute-start(f32[49,8,128]{2,1,0:T(8,128)S(1)} %pack.1.own), channel_id=1, source_target_pairs={{0,1},{1,2},{2,3},{3,4},{4,5},{5,6},{6,7},{7,0},{8,9},{9,10},{10,1... | collective-permute-start | bytes 602120 | tf_op jit(solution)/shard_map/ppermute | solution.py:341
  18.0 8.6 %collective-permute-start.2 = (f32[27,8,384]{2,1,0:T(8,128)S(1)}, f32[27,8,384]{2,1,0:T(8,128)S(1)}, u32[]{:S(2)}, u32[]{:S(2)}) collective-permute-start(f32[27,8,384]{2,1,0:T(8,128)S(1)} %get-tuple-element.24), channel_id=1, source_target_pairs={{0,8},{8,16},{16,24},{24,32},{32,40},{40,48},{48,56},{56,64},{64,7... | collective-permute-start | bytes 995336 | tf_op jit(solution)/shard_map/ppermute | solution.py:341
  22.3 9.6 %collective-permute-start.3 = (f32[27,8,384]{2,1,0:T(8,128)S(1)}, f32[27,8,384]{2,1,0:T(8,128)S(1)}, u32[]{:S(2)}, u32[]{:S(2)}) collective-permute-start(f32[27,8,384]{2,1,0:T(8,128)S(1)} %get-tuple-element.25), channel_id=1, source_target_pairs={{0,120},{8,0},{16,8},{24,16},{32,24},{40,32},{48,40},{56,48},{64,5... | collective-permute-start | bytes 995336 | tf_op jit(solution)/shard_map/ppermute | solution.py:341
  32.7 2.4 %collective-permute-start.4 = (f32[336,128]{1,0:T(8,128)S(1)}, f32[336,128]{1,0:T(8,128)S(1)}, u32[]{:S(2)}, u32[]{:S(2)}) collective-permute-start(f32[336,128]{1,0:T(8,128)S(1)} %get-tuple-element.29), channel_id=1, source_target_pairs={{0,8},{8,16},{16,24},{24,32},{32,40},{40,48},{48,56},{56,64},{64,7... | collective-permute-start | bytes 516104 | tf_op jit(solution)/shard_map/ppermute | solution.py:341
  32.8 6.4 %collective-permute-start.5 = (f32[336,128]{1,0:T(8,128)S(1)}, f32[336,128]{1,0:T(8,128)S(1)}, u32[]{:S(2)}, u32[]{:S(2)}) collective-permute-start(f32[336,128]{1,0:T(8,128)S(1)} %get-tuple-element.30), channel_id=1, source_target_pairs={{0,120},{8,0},{16,8},{24,16},{32,24},{40,32},{48,40},{56,48},{64,5... | collective-permute-start | bytes 516104 | tf_op jit(solution)/shard_map/ppermute | solution.py:341
  39.8 7.4 %collective-permute-start.6 = (f32[288,128]{1,0:T(8,128)S(1)}, f32[288,128]{1,0:T(8,128)S(1)}, u32[]{:S(2)}, u32[]{:S(2)}) collective-permute-start(f32[288,128]{1,0:T(8,128)S(1)} %get-tuple-element.32), channel_id=1, source_target_pairs={{0,8},{8,16},{16,24},{24,32},{32,40},{40,48},{48,56},{56,64},{64,7... | collective-permute-start | bytes 442376 | tf_op jit(solution)/shard_map/ppermute | solution.py:341
  45.1 7.6 %collective-permute-start.7 = (f32[288,128]{1,0:T(8,128)S(1)}, f32[288,128]{1,0:T(8,128)S(1)}, u32[]{:S(2)}, u32[]{:S(2)}) collective-permute-start(f32[288,128]{1,0:T(8,128)S(1)} %get-tuple-element.33), channel_id=1, source_target_pairs={{0,120},{8,0},{16,8},{24,16},{32,24},{40,32},{48,40},{56,48},{64,5... | collective-permute-start | bytes 442376 | tf_op jit(solution)/shard_map/ppermute | solution.py:341
  53.3 1.9 %collective-permute-start.8 = (f32[240,128]{1,0:T(8,128)S(1)}, f32[240,128]{1,0:T(8,128)S(1)}, u32[]{:S(2)}, u32[]{:S(2)}) collective-permute-start(f32[240,128]{1,0:T(8,128)S(1)} %get-tuple-element.35), channel_id=1, source_target_pairs={{0,8},{8,16},{16,24},{24,32},{32,40},{40,48},{48,56},{56,64},{64,7... | collective-permute-start | bytes 368648 | tf_op jit(solution)/shard_map/ppermute | solution.py:341
  53.4 7.4 %collective-permute-start.9 = (f32[240,128]{1,0:T(8,128)S(1)}, f32[240,128]{1,0:T(8,128)S(1)}, u32[]{:S(2)}, u32[]{:S(2)}) collective-permute-start(f32[240,128]{1,0:T(8,128)S(1)} %get-tuple-element.36), channel_id=1, source_target_pairs={{0,120},{8,0},{16,8},{24,16},{32,24},{40,32},{48,40},{56,48},{64,5... | collective-permute-start | bytes 368648 | tf_op jit(solution)/shard_map/ppermute | solution.py:341
  65.7 1.7 %collective-permute-start.10 = (f32[192,128]{1,0:T(8,128)S(1)}, f32[192,128]{1,0:T(8,128)S(1)}, u32[]{:S(2)}, u32[]{:S(2)}) collective-permute-start(f32[192,128]{1,0:T(8,128)S(1)} %get-tuple-element.38), channel_id=1, source_target_pairs={{0,8},{8,16},{16,24},{24,32},{32,40},{40,48},{48,56},{56,64},{64,7... | collective-permute-start | bytes 294920 | tf_op jit(solution)/shard_map/ppermute | solution.py:341
  65.8 6.6 %collective-permute-start.11 = (f32[192,128]{1,0:T(8,128)S(1)}, f32[192,128]{1,0:T(8,128)S(1)}, u32[]{:S(2)}, u32[]{:S(2)}) collective-permute-start(f32[192,128]{1,0:T(8,128)S(1)} %get-tuple-element.39), channel_id=1, source_target_pairs={{0,120},{8,0},{16,8},{24,16},{32,24},{40,32},{48,40},{56,48},{64,5... | collective-permute-start | bytes 294920 | tf_op jit(solution)/shard_map/ppermute | solution.py:341
  72.3 9.7 %copy-start.1 = (f32[2,8,8,128]{3,2,1,0:T(8,128)S(1)}, f32[2,8,8,128]{3,2,1,0:T(8,128)}, u32[]{:S(2)}) copy-start(f32[2,8,8,128]{3,2,1,0:T(8,128)} %basis.7) | copy-start | bytes 196612
  72.3 9.7 %copy-start.3 = (f32[3,8,8,128]{3,2,1,0:T(8,128)S(1)}, f32[3,8,8,128]{3,2,1,0:T(8,128)}, u32[]{:S(2)}) copy-start(f32[3,8,8,128]{3,2,1,0:T(8,128)} %mix.3) | copy-start | bytes 294916
  72.3 9.7 %copy-start.5 = (f32[2,8,8,128]{3,2,1,0:T(8,128)S(1)}, f32[2,8,8,128]{3,2,1,0:T(8,128)}, u32[]{:S(2)}) copy-start(f32[2,8,8,128]{3,2,1,0:T(8,128)} %forc.3) | copy-start | bytes 196612
  72.4 9.7 %copy-start.7 = (s32[8,8,128]{2,1,0:T(8,128)S(1)}, s32[8,8,128]{2,1,0:T(8,128)}, u32[]{:S(2)}) copy-start(s32[8,8,128]{2,1,0:T(8,128)} %lab.3) | copy-start | bytes 98308
  75.0 1.5 %collective-permute-start.12 = (f32[144,128]{1,0:T(8,128)S(1)}, f32[144,128]{1,0:T(8,128)S(1)}, u32[]{:S(2)}, u32[]{:S(2)}) collective-permute-start(f32[144,128]{1,0:T(8,128)S(1)} %get-tuple-element.41), channel_id=1, source_target_pairs={{0,8},{8,16},{16,24},{24,32},{32,40},{40,48},{48,56},{56,64},{64,7... | collective-permute-start | bytes 221192 | tf_op jit(solution)/shard_map/ppermute | solution.py:341
  75.1 6.9 %collective-permute-start.13 = (f32[144,128]{1,0:T(8,128)S(1)}, f32[144,128]{1,0:T(8,128)S(1)}, u32[]{:S(2)}, u32[]{:S(2)}) collective-permute-start(f32[144,128]{1,0:T(8,128)S(1)} %get-tuple-element.42), channel_id=1, source_target_pairs={{0,120},{8,0},{16,8},{24,16},{32,24},{40,32},{48,40},{56,48},{64,5... | collective-permute-start | bytes 221192 | tf_op jit(solution)/shard_map/ppermute | solution.py:341
  82.7 28.9 %copy-start.8 = (f32[1,1,2,256]{3,2,1,0:T(2,128)S(1)}, f32[1,1,2,256]{3,2,1,0:T(2,128)}, u32[]{:S(2)}) copy-start(f32[1,1,2,256]{3,2,1,0:T(2,128)} %inv.1) | copy-start | bytes 6148
